TPU v7x, 256 devices: a whole 4x4x8 slice. The times are simulated.
256 devices in a mesh: ctx: 32 (over z, y_hi, core), head: 8 (over x, y_lo).
Axes of the slice: x: 4, y: 4 (y_hi: 2, y_lo: 2; y = y_hi * 2 + y_lo), z: 8, core: 2. Of those that a mesh axis runs over, the one named last changes fastest.
Arguments:
- queries: bfloat16 [20480, 2048], P('ctx', 'head'), may hold values from -8 to 8
- keys: bfloat16 [20480, 2048], P('ctx', 'head'), may hold values from -6 to 6
- values: bfloat16 [20480, 2048], P('ctx', 'head'), may hold values from -6 to 6
- key_weight: bfloat16 [16, 16, 128], P('head'), may hold values from -1.5 to 1.5
- value_weight: bfloat16 [16, 16, 128], P('head'), may hold values from -1.5 to 1.5
Outputs:
- attended: bfloat16 [20480, 2048], P(('ctx', 'head'))
All inputs are finite; a program needn't handle non-finite values.
Results may differ from a plain program's by a relative error of at most 0.0061.
Values may be sent and summed in bfloat16 or wider, within the bound.
No kernel may reach another device: no remote copies, remote signals or barrier semaphores. Data moves between devices by JAX's collectives and lax.ppermute only.
A program may use at most 64 MiB of HBM per device.

v0:
```python
import math
import jax
import jax.numpy as jnp
from jax import lax
from jax.sharding import PartitionSpec as P

query_span = 512
key_span = 1024


def from_partner(shard, axis, stride):
    return lax.ppermute(shard, axis, [(i, i ^ 1 << stride) for i in range(lax.axis_size(axis))])


def fold_rows(values_in, weight):
    row_count, channels = values_in.shape
    head_count, group_size, head_width = weight.shape
    grouped = values_in.reshape(row_count // group_size, group_size, head_count, head_width)
    folded = jnp.einsum("gjhd,hjd->ghd", grouped, weight, preferred_element_type=jnp.float32)
    return folded.astype(jnp.bfloat16).reshape(row_count // group_size, channels)


def attend(carried, query_heads, key_rows, value_rows):
    top_now, total_now, summed = carried
    query_count, head_count, head_width = query_heads.shape
    key_count = key_rows.shape[0]
    key_heads = key_rows.reshape(key_count, head_count, head_width)
    value_heads = value_rows.reshape(key_count, head_count, head_width)
    score_scale = 1.0 / math.sqrt(head_width)
    top_parts, total_parts, sum_parts = ([], [], [])
    for query_start in range(0, query_count, query_span):
        query_end = min(query_count, query_start + query_span)
        run_top = top_now[:, query_start:query_end]
        run_total = total_now[:, query_start:query_end]
        run_sum = summed[:, query_start:query_end]
        for key_start in range(0, key_count, key_span):
            key_end = min(key_count, key_start + key_span)
            scores = (
                jnp.einsum(
                    "qhd,khd->hqk",
                    query_heads[query_start:query_end],
                    key_heads[key_start:key_end],
                    preferred_element_type=jnp.float32,
                )
                * score_scale
            )
            new_top = jnp.maximum(run_top, jnp.max(scores, axis=2))
            factor = jnp.exp(run_top - new_top)
            weights = jnp.exp(scores - new_top[:, :, None])
            run_total = run_total * factor + jnp.sum(weights, axis=2)
            run_sum = run_sum * factor[:, :, None] + jnp.einsum(
                "hqk,khd->hqd",
                weights.astype(jnp.bfloat16),
                value_heads[key_start:key_end],
                preferred_element_type=jnp.float32,
            )
            run_top = new_top
        top_parts.append(run_top)
        total_parts.append(run_total)
        sum_parts.append(run_sum)
    return (
        jnp.concatenate(top_parts, 1),
        jnp.concatenate(total_parts, 1),
        jnp.concatenate(sum_parts, 1),
    )


def body(queries, keys, values, key_weight, value_weight):
    block_rows, channels = queries.shape
    head_count, group_size, head_width = key_weight.shape
    query_heads = queries.reshape(block_rows, head_count, head_width)
    folded_keys = fold_rows(keys, key_weight)
    folded_values = fold_rows(values, value_weight)
    carried = (
        jnp.full((head_count, block_rows), -jnp.inf, jnp.float32),
        jnp.zeros((head_count, block_rows), jnp.float32),
        jnp.zeros((head_count, block_rows, head_width), jnp.float32),
    )
    carried = attend(carried, query_heads, keys, values)
    bit_count = lax.axis_size("ctx").bit_length() - 1
    for bit_index in range(bit_count):
        far_keys, far_values = from_partner((keys, values), "ctx", bit_index)
        carried = attend(carried, query_heads, far_keys, far_values)
    carried = attend(
        carried,
        query_heads,
        lax.all_gather(folded_keys, "ctx", axis=0, tiled=True),
        lax.all_gather(folded_values, "ctx", axis=0, tiled=True),
    )
    top_now, total_now, summed = carried
    result = (summed / total_now[:, :, None]).astype(jnp.bfloat16)
    result = jnp.transpose(result, (1, 0, 2)).reshape(block_rows, head_count * head_width)
    return lax.all_to_all(result, "head", split_axis=0, concat_axis=1, tiled=True)


def solution(mesh):
    in_specs = (
        P("ctx", "head"),
        P("ctx", "head"),
        P("ctx", "head"),
        P("head", None, None),
        P("head", None, None),
    )
    out_specs = P(("ctx", "head"), None)
    return jax.shard_map(body, mesh=mesh, in_specs=in_specs, out_specs=out_specs, check_vma=False)
```

profile of v0, /device:TPU:16, one launch (start us, length us, event | category | flops | bytes accessed | tf_op | source)
XLA Modules:
  0.0 195.2 jit_solution(15290584683478375523)
XLA Ops:
  0.0 1.9 copy.149
  1.9 7.2 %collective-permute-start.8 = (bf16[640,256]{0,1:T(8,128)(2,1)}, bf16[640,256]{0,1:T(8,128)(2,1)}, u32[]{:S(2)}, u32[]{:S(2)}) collective-permute-start(bf16[640,256]{0,1:T(8,128)(2,1)} %copy.149), channel_id=1, source_target_pairs={{0,128},{8,136},{16,144},{24,152},{32,160},{40,168},{48,176},{56,1... | collective-permute-start | bytes 983048 | tf_op jit(solution)/shard_map/ppermute | solution.py:12
  9.1 1.5 collective-permute-start.6
  14.1 56.2 %all_gather.6 = bf16[1280,256]{1,0:T(8,128)(2,1)S(1)} all-gather(bf16[40,256]{1,0:T(8,128)(2,1)S(1)} %bitcast.164), channel_id=1, replica_groups=mesh['ctx'=32,'head'=8] {'ctx'}, dimensions={0}, use_global_device_ids=true | all-gather | bytes 675840 | tf_op jit(solution)/shard_map/all_gather | solution.py:87
  73.0 2.7 %bitcast_reduce_fusion = (f32[2,512]{1,0:T(2,128)S(1)}, f32[2,1024,512]{2,1,0:T(8,128)}) fusion(bf16[1024,2,128]{0,2,1:T(8,128)(2,1)S(1)} %bitcast.146, bf16[512,2,128]{0,2,1:T(8,128)(2,1)S(1)} %bitcast.127), kind=kOutput, calls=%fused_computation.1 | convolution fusion | flops 270531584 | bytes 4984832 | tf_op jit(solution)/shard_map/qhd,khd->hqk/dot_general | solution.py:39
  76.1 1.8 reshape.409
  80.0 43.2 %all_gather.7 = bf16[1280,256]{1,0:T(8,128)(2,1)} all-gather(bf16[40,256]{1,0:T(8,128)(2,1)S(1)} %bitcast.165), channel_id=1, replica_groups=mesh['ctx'=32,'head'=8] {'ctx'}, dimensions={0}, use_global_device_ids=true | all-gather | bytes 675840 | tf_op jit(solution)/shard_map/all_gather | solution.py:88
  123.2 1.9 fusion.167
  125.1 1.9 copy.152
  126.9 1.9 slice.85
  128.8 2.0 %copy.279 = bf16[1024,256]{0,1:T(8,128)(2,1)} copy(bf16[1024,256]{1,0:T(8,128)(2,1)} %slice.85) | data formatting | bytes 1048576
  132.6 1.5 collective-permute-start.9
  135.5 1.6 multiply_reduce_fusion
  137.4 1.4 fusion.170
  138.7 1.6 multiply_reduce_fusion.1
  140.4 2.9 %collective-permute-start.5 = (bf16[640,256]{0,1:T(8,128)(2,1)S(1)}, bf16[640,256]{0,1:T(8,128)(2,1)S(1)}, u32[]{:S(2)}, u32[]{:S(2)}) collective-permute-start(bf16[640,256]{0,1:T(8,128)(2,1)S(1)} %copy-done.8), channel_id=1, source_target_pairs={{0,32},{8,40},{16,48},{24,56},{32,0},{40,8},{48,16},{56,24},{64,96... | collective-permute-start | bytes 983048 | tf_op jit(solution)/shard_map/ppermute | solution.py:12
  143.3 1.4 fusion.171
  144.7 1.6 multiply_reduce_fusion.2
  148.8 1.6 multiply_reduce_fusion.3
  150.6 1.6 multiply_reduce_fusion.4
  152.2 1.4 fusion.174
  156.3 9.2 %collective-permute-done.7 = bf16[640,256]{0,1:T(8,128)(2,1)S(1)} collective-permute-done((bf16[640,256]{0,1:T(8,128)(2,1)S(1)}, bf16[640,256]{0,1:T(8,128)(2,1)S(1)}, u32[]{:S(2)}, u32[]{:S(2)}) %collective-permute-start.7) | collective-permute-done | bytes 327712 | tf_op jit(solution)/shard_map/ppermute | solution.py:12
  177.9 1.5 fusion.87
  180.6 13.9 %all_to_all.19 = bf16[8,80,256]{2,1,0:T(8,128)(2,1)S(1)} all-to-all(bf16[8,80,256]{2,1,0:T(8,128)(2,1)S(1)} %all_to_all.14), channel_id=1, replica_groups=mesh['ctx'=32,'head'=8] {'head'}, dimensions={0} | all-to-all | bytes 655360 | tf_op jit(solution)/shard_map/all_to_all | solution.py:93
  (98 shorter events, 31.5 us)
Async XLA Ops:
  0.0 71.1 %slice-start.2 = ((bf16[640,256]{1,0:T(8,128)(2,1)}), bf16[512,256]{1,0:T(8,128)(2,1)S(1)}, s32[]{:S(2)}) async-start(bf16[640,256]{1,0:T(8,128)(2,1)} %param.5), calls=%async_computation.3 | async-start | bytes 524288 | tf_op jit(solution)/shard_map/slice | solution.py:41
  1.9 69.6 %slice-start.3 = ((bf16[640,256]{1,0:T(8,128)(2,1)}), bf16[128,256]{1,0:T(8,128)(2,1)S(1)}, s32[]{:S(2)}) async-start(bf16[640,256]{1,0:T(8,128)(2,1)} %param.5), calls=%async_computation.4 | async-start | bytes 131072 | tf_op jit(solution)/shard_map/slice | solution.py:41
  1.9 69.7 %copy-start.1 = (bf16[640,256]{1,0:T(8,128)(2,1)S(1)}, bf16[640,256]{1,0:T(8,128)(2,1)}, u32[]{:S(2)}) copy-start(bf16[640,256]{1,0:T(8,128)(2,1)} %param.6) | copy-start | bytes 983044
  1.9 130.4 %collective-permute-start.8 = (bf16[640,256]{0,1:T(8,128)(2,1)}, bf16[640,256]{0,1:T(8,128)(2,1)}, u32[]{:S(2)}, u32[]{:S(2)}) collective-permute-start(bf16[640,256]{0,1:T(8,128)(2,1)} %copy.149), channel_id=1, source_target_pairs={{0,128},{8,136},{16,144},{24,152},{32,160},{40,168},{48,176},{56,1... | collective-permute-start | bytes 983048 | tf_op jit(solution)/shard_map/ppermute | solution.py:12
  9.1 128.0 %collective-permute-start.6 = (bf16[640,256]{0,1:T(8,128)(2,1)}, bf16[640,256]{0,1:T(8,128)(2,1)}, u32[]{:S(2)}, u32[]{:S(2)}) collective-permute-start(bf16[640,256]{0,1:T(8,128)(2,1)} %copy.149), channel_id=1, source_target_pairs={{0,64},{8,72},{16,80},{24,88},{32,96},{40,104},{48,112},{56,120},{... | collective-permute-start | bytes 983048 | tf_op jit(solution)/shard_map/ppermute | solution.py:12
  10.6 129.8 %collective-permute-start.4 = (bf16[640,256]{0,1:T(8,128)(2,1)}, bf16[640,256]{0,1:T(8,128)(2,1)}, u32[]{:S(2)}, u32[]{:S(2)}) collective-permute-start(bf16[640,256]{0,1:T(8,128)(2,1)} %copy.149), channel_id=1, source_target_pairs={{0,32},{8,40},{16,48},{24,56},{32,0},{40,8},{48,16},{56,24},{64,96... | collective-permute-start | bytes 983048 | tf_op jit(solution)/shard_map/ppermute | solution.py:12
  11.6 134.7 %collective-permute-start.2 = (bf16[640,256]{0,1:T(8,128)(2,1)}, bf16[640,256]{0,1:T(8,128)(2,1)}, u32[]{:S(2)}, u32[]{:S(2)}) collective-permute-start(bf16[640,256]{0,1:T(8,128)(2,1)} %copy.149), channel_id=1, source_target_pairs={{0,16},{8,24},{16,0},{24,8},{32,48},{40,56},{48,32},{56,40},{64,80... | collective-permute-start | bytes 983048 | tf_op jit(solution)/shard_map/ppermute | solution.py:12
  11.9 138.5 %collective-permute-start = (bf16[640,256]{0,1:T(8,128)(2,1)}, bf16[640,256]{0,1:T(8,128)(2,1)}, u32[]{:S(2)}, u32[]{:S(2)}) collective-permute-start(bf16[640,256]{0,1:T(8,128)(2,1)} %copy.149), channel_id=1, source_target_pairs={{0,8},{8,0},{16,24},{24,16},{32,40},{40,32},{48,56},{56,48},{64,72... | collective-permute-start | bytes 983048 | tf_op jit(solution)/shard_map/ppermute | solution.py:12
  70.3 0.8 copy-start.4
  73.0 2.7 %slice-start.1 = ((bf16[1280,256]{1,0:T(8,128)(2,1)}), bf16[256,256]{1,0:T(8,128)(2,1)S(1)}, s32[]{:S(2)}) async-start(bf16[1280,256]{1,0:T(8,128)(2,1)} %copy-done.4), calls=%async_computation.2 | async-start | bytes 262144 | tf_op jit(solution)/shard_map/slice | solution.py:42
  75.7 4.2 %copy-start.6 = (bf16[256,256]{0,1:T(8,128)(2,1)}, bf16[256,256]{0,1:T(8,128)(2,1)S(1)}, u32[]{:S(2)}) copy-start(bf16[256,256]{0,1:T(8,128)(2,1)S(1)} %copy.280) | copy-start | bytes 393220
  123.2 7.7 %slice-start = ((bf16[1280,256]{1,0:T(8,128)(2,1)}), bf16[256,256]{1,0:T(8,128)(2,1)S(1)}, s32[]{:S(2)}) async-start(bf16[1280,256]{1,0:T(8,128)(2,1)} %all_gather.7), calls=%async_computation.1 | async-start | bytes 262144 | tf_op jit(solution)/shard_map/slice | solution.py:54
  131.6 1.0 copy-start.8
  132.6 35.3 %collective-permute-start.9 = (bf16[640,256]{0,1:T(8,128)(2,1)S(1)}, bf16[640,256]{0,1:T(8,128)(2,1)S(1)}, u32[]{:S(2)}, u32[]{:S(2)}) collective-permute-start(bf16[640,256]{0,1:T(8,128)(2,1)S(1)} %copy-done.8), channel_id=1, source_target_pairs={{0,128},{8,136},{16,144},{24,152},{32,160},{40,168},{48,176},{56,1... | collective-permute-start | bytes 983048 | tf_op jit(solution)/shard_map/ppermute | solution.py:12
  137.1 28.4 %collective-permute-start.7 = (bf16[640,256]{0,1:T(8,128)(2,1)S(1)}, bf16[640,256]{0,1:T(8,128)(2,1)S(1)}, u32[]{:S(2)}, u32[]{:S(2)}) collective-permute-start(bf16[640,256]{0,1:T(8,128)(2,1)S(1)} %copy-done.8), channel_id=1, source_target_pairs={{0,64},{8,72},{16,80},{24,88},{32,96},{40,104},{48,112},{56,120},{... | collective-permute-start | bytes 983048 | tf_op jit(solution)/shard_map/ppermute | solution.py:12
  140.4 26.2 %collective-permute-start.5 = (bf16[640,256]{0,1:T(8,128)(2,1)S(1)}, bf16[640,256]{0,1:T(8,128)(2,1)S(1)}, u32[]{:S(2)}, u32[]{:S(2)}) collective-permute-start(bf16[640,256]{0,1:T(8,128)(2,1)S(1)} %copy-done.8), channel_id=1, source_target_pairs={{0,32},{8,40},{16,48},{24,56},{32,0},{40,8},{48,16},{56,24},{64,96... | collective-permute-start | bytes 983048 | tf_op jit(solution)/shard_map/ppermute | solution.py:12
  146.3 27.3 %collective-permute-start.3 = (bf16[640,256]{0,1:T(8,128)(2,1)S(1)}, bf16[640,256]{0,1:T(8,128)(2,1)S(1)}, u32[]{:S(2)}, u32[]{:S(2)}) collective-permute-start(bf16[640,256]{0,1:T(8,128)(2,1)S(1)} %copy-done.8), channel_id=1, source_target_pairs={{0,16},{8,24},{16,0},{24,8},{32,48},{40,56},{48,32},{56,40},{64,80... | collective-permute-start | bytes 983048 | tf_op jit(solution)/shard_map/ppermute | solution.py:12
  150.5 27.4 %collective-permute-start.1 = (bf16[640,256]{0,1:T(8,128)(2,1)S(1)}, bf16[640,256]{0,1:T(8,128)(2,1)S(1)}, u32[]{:S(2)}, u32[]{:S(2)}) collective-permute-start(bf16[640,256]{0,1:T(8,128)(2,1)S(1)} %copy-done.8), channel_id=1, source_target_pairs={{0,8},{8,0},{16,24},{24,16},{32,40},{40,32},{48,56},{56,48},{64,72... | collective-permute-start | bytes 983048 | tf_op jit(solution)/shard_map/ppermute | solution.py:12
  153.6 1.4 copy-start.9
  167.9 0.9 copy-start.7
  168.8 1.2 copy-start.2
  169.2 2.2 %copy-start = (f32[2,1024,512]{2,1,0:T(8,128)S(1)}, f32[2,1024,512]{2,1,0:T(8,128)}, u32[]{:S(2)}) copy-start(f32[2,1024,512]{2,1,0:T(8,128)} %get-tuple-element.56) | copy-start | bytes 12582916
  171.5 1.2 copy-start.5
  174.3 2.1 %copy-start.3 = (bf16[640,256]{1,0:T(8,128)(2,1)S(1)}, bf16[640,256]{1,0:T(8,128)(2,1)}, u32[]{:S(2)}) copy-start(bf16[640,256]{1,0:T(8,128)(2,1)} %param.7) | copy-start | bytes 983044
where the time goes:
time: 196 us; the launch traced here: 195 us
  blocking collectives  113 us (58%)
  matrix products  31.2 us (16%)
  starting transfers between devices  16 us (8%)
  local copies, waits for them, and re-layouts  15.4 us (8%)
  other arithmetic  9.62 us (5%)
  waiting for transfers between devices  9.24 us (5%)
    all_gather x1, blocking collectives, body(): lax.all_gather(folded_keys, 'ctx', axis=0, tiled=True)  56.2 us
    all_gather x1, blocking collectives, body(): lax.all_gather(folded_values, 'ctx', axis=0, tiled=True)  43.2 us
    dot_general x16, matrix products, attend(): jnp.einsum('qhd,khd->hqk', query_heads[query_start:query_end], key_heads[...  21.8 us
    ppermute x10, starting transfers between devices, from_partner(): lax.ppermute(shard, axis, [(i, i ^ 1 << stride) for i in range(lax.axis_s...  16 us
    all_to_all x1, blocking collectives, body(): lax.all_to_all(result, 'head', split_axis=0, concat_axis=1, tiled=True)  13.9 us
    dot_general x16, matrix products, attend(): jnp.einsum('hqk,khd->hqd', weights.astype(jnp.bfloat16), value_heads[key_...  9.46 us
    unnamed x32, local copies, waits for them, and re-layouts  9.32 us
    ppermute x10, waiting for transfers between devices, from_partner(): lax.ppermute(shard, axis, [(i, i ^ 1 << stride) for i in range(lax.axis_s...  9.24 us
  transfers between devices with their start and end apart: 10, of which 1 were waited for; matrix products, arithmetic and copies ran while one was open for 25% of the time, Pallas kernels for 0%

commit v1 on v0

--- a/solution.py
+++ b/solution.py
@@ -6,6 +6,19 @@
 
 query_span = 512
 key_span = 1024
+
+
+def see_strings(block_here):
+    p_next = jnp.concatenate(
+        lax.all_to_all(
+            jnp.stack([block_here] * lax.psum(1, axis_name="ctx")),
+            axis_name="ctx",
+            split_axis=0,
+            concat_axis=0,
+        ),
+        axis=0,
+    )
+    return p_next
 
 
 def from_partner(shard, axis, stride):
@@ -85,7 +98,7 @@
         carried,
         query_heads,
         lax.all_gather(folded_keys, "ctx", axis=0, tiled=True),
-        lax.all_gather(folded_values, "ctx", axis=0, tiled=True),
+        see_strings(folded_values),
     )
     top_now, total_now, summed = carried
     result = (summed / total_now[:, :, None]).astype(jnp.bfloat16)

time: 196 us -> 177 us (0.903)
  blocking collectives: 113 us -> 74.2 us
  matrix products: 31.2 us -> 42.2 us
  starting transfers between devices: 16 us -> 23.7 us
  local copies, waits for them, and re-layouts: 15.4 us -> 13.1 us
  waiting for transfers between devices: 9.24 us -> 11.5 us
    all_gather x1 -> x0, blocking collectives: 43.2 us -> none  [body(): lax.all_gather(folded_values, 'ctx', axis=0, tiled=True)]
    dot_general x16, matrix products: 9.46 us -> 21.6 us  [attend(): jnp.einsum('hqk,khd->hqd', weights.astype(jnp.bfloat16), value_heads[key_...]
    all_to_all x0 -> x1, starting transfers between devices: none -> 7.53 us  [see_strings(): lax.all_to_all(jnp.stack([block_here] * lax.psum(1, axis_name='ctx')), ax...]
    all_gather x1, blocking collectives: 56.2 us -> 61.3 us  [body(): lax.all_gather(folded_keys, 'ctx', axis=0, tiled=True)]
    unnamed x32 -> x94, local copies, waits for them, and re-layouts: 9.32 us -> 4.61 us
    another operation x0 -> x2, local copies, waits for them, and re-layouts: none -> 3.41 us  [the longest x1 2.52 us: attend(): value_heads = value_rows.reshape(key_count, head_count, head_width)]
    ppermute x10, waiting for transfers between devices: 9.24 us -> 11.5 us  [from_partner(): lax.ppermute(shard, axis, [(i, i ^ 1 << stride) for i in range(lax.axis_s...]
  transfers between devices with their start and end apart: 10 -> 11, of which waited for: 1 -> 2; matrix products, arithmetic and copies ran while one was open for 25% -> 32% of each run, Pallas kernels for 0% -> 0%
where the time goes in v1:
time: 177 us; the launch traced here: 175 us
  blocking collectives  74.2 us (42%)
  matrix products  42.2 us (24%)
  starting transfers between devices  23.7 us (13%)
  local copies, waits for them, and re-layouts  13.1 us (7%)
  waiting for transfers between devices  11.5 us (6%)
  other arithmetic  9.69 us (5%)
    all_gather x1, blocking collectives, body(): lax.all_gather(folded_keys, 'ctx', axis=0, tiled=True)  61.3 us
    dot_general x16, matrix products, attend(): jnp.einsum('hqk,khd->hqd', weights.astype(jnp.bfloat16), value_heads[key_...  21.6 us
    dot_general x16, matrix products, attend(): jnp.einsum('qhd,khd->hqk', query_heads[query_start:query_end], key_heads[...  20.6 us
    ppermute x10, starting transfers between devices, from_partner(): lax.ppermute(shard, axis, [(i, i ^ 1 << stride) for i in range(lax.axis_s...  16.2 us
    all_to_all x1, blocking collectives, body(): lax.all_to_all(result, 'head', split_axis=0, concat_axis=1, tiled=True)  12.9 us
    ppermute x10, waiting for transfers between devices, from_partner(): lax.ppermute(shard, axis, [(i, i ^ 1 << stride) for i in range(lax.axis_s...  11.5 us
    all_to_all x1, starting transfers between devices, see_strings(): lax.all_to_all(jnp.stack([block_here] * lax.psum(1, axis_name='ctx')), ax...  7.53 us
    reduce_sum x10, other arithmetic, attend(): run_total = run_total * factor + jnp.sum(weights, axis=2)  6.15 us
  transfers between devices with their start and end apart: 11, of which 2 were waited for; matrix products, arithmetic and copies ran while one was open for 32% of the time, Pallas kernels for 0%

profile of v1, /device:TPU:16, one launch (start us, length us, event | category | flops | bytes accessed | tf_op | source)
XLA Modules:
  0.0 175.2 jit_solution(4421675616270305893)
XLA Ops:
  0.0 1.9 %copy.146 = bf16[640,256]{0,1:T(8,128)(2,1)} copy(bf16[640,256]{1,0:T(8,128)(2,1)} %param.6) | data formatting | bytes 655360 | tf_op args[1]
  1.9 7.2 %collective-permute-start.8 = (bf16[640,256]{0,1:T(8,128)(2,1)}, bf16[640,256]{0,1:T(8,128)(2,1)}, u32[]{:S(2)}, u32[]{:S(2)}) collective-permute-start(bf16[640,256]{0,1:T(8,128)(2,1)} %copy.146), channel_id=1, source_target_pairs={{0,128},{8,136},{16,144},{24,152},{32,160},{40,168},{48,176},{56,1... | collective-permute-start | bytes 983048 | tf_op jit(solution)/shard_map/ppermute | solution.py:25
  9.1 1.5 collective-permute-start.6
  15.0 7.5 %all-to-all-start = ((bf16[32,40,256]{2,1,0:T(8,128)(2,1)}), bf16[32,40,256]{2,1,0:T(8,128)(2,1)}, u32[]{:S(2)}, u32[]{:S(2)}) async-start(bf16[32,40,256]{2,1,0:T(8,128)(2,1)} %stack.3), calls=%async_computation | async-start | bytes 1310720 | tf_op jit(solution)/shard_map/all_to_all | solution.py:13
  23.1 61.3 %all_gather.3 = bf16[1280,256]{1,0:T(8,128)(2,1)S(1)} all-gather(bf16[40,256]{1,0:T(8,128)(2,1)S(1)} %bitcast.157), channel_id=1, replica_groups=mesh['ctx'=32,'head'=8] {'ctx'}, dimensions={0}, use_global_device_ids=true | all-gather | bytes 675840 | tf_op jit(solution)/shard_map/all_gather | solution.py:100
  86.7 3.3 %bitcast_reduce_fusion = (f32[2,512]{1,0:T(2,128)}, f32[2,1024,512]{2,1,0:T(8,128)}) fusion(bf16[1024,2,128]{0,2,1:T(8,128)(2,1)S(1)} %bitcast.138, bf16[512,2,128]{0,2,1:T(8,128)(2,1)S(1)} %bitcast.121), kind=kOutput, calls=%fused_computation.1 | convolution fusion | flops 270531584 | bytes 4984832 | tf_op jit(solution)/shard_map/qhd,khd->hqk/dot_general | solution.py:52
  90.0 1.9 %fusion.179 = (f32[2,512]{1,0:T(2,128)}, f32[2,512,256]{1,2,0:T(8,128)}) fusion(bf16[256,2,128]{0,2,1:T(8,128)(2,1)S(1)} %bitcast.152, bf16[512,2,128]{0,2,1:T(8,128)(2,1)S(1)} %bitcast.122), kind=kOutput, calls=%fused_computation.193 | convolution fusion | flops 67632128 | bytes 1445888 | tf_op jit(solution)/shard_map/qhd,khd->hqk/dot_general | solution.py:52
  94.5 3.8 %collective-permute-start.9 = (bf16[640,256]{0,1:T(8,128)(2,1)}, bf16[640,256]{0,1:T(8,128)(2,1)S(1)}, u32[]{:S(2)}, u32[]{:S(2)}) collective-permute-start(bf16[640,256]{0,1:T(8,128)(2,1)} %copy.149), channel_id=1, source_target_pairs={{0,128},{8,136},{16,144},{24,152},{32,160},{40,168},{48,176},{56,1... | collective-permute-start | bytes 983048 | tf_op jit(solution)/shard_map/ppermute | solution.py:25
  99.7 1.6 multiply_reduce_fusion
  102.8 1.6 multiply_reduce_fusion.1
  106.5 1.6 multiply_reduce_fusion.2
  108.2 1.4 collective-permute-start.3
  117.3 10.4 %collective-permute-done.7 = bf16[640,256]{0,1:T(8,128)(2,1)S(1)} collective-permute-done((bf16[640,256]{0,1:T(8,128)(2,1)}, bf16[640,256]{0,1:T(8,128)(2,1)S(1)}, u32[]{:S(2)}, u32[]{:S(2)}) %collective-permute-start.7) | collective-permute-done | bytes 327712 | tf_op jit(solution)/shard_map/ppermute | solution.py:25
  129.0 1.5 fusion.21
  139.6 1.5 fusion.23
  141.1 1.6 fusion.25
  142.6 1.5 fusion.27
  144.1 1.6 fusion.48
  145.7 2.5 %reshape_reshape.3 = bf16[1280,2,128]{2,1,0:T(2,128)(2,1)} reshape(bf16[32,40,256]{2,1,0:T(8,128)(2,1)} %all-to-all-done) | data formatting | bytes 1310720 | tf_op jit(solution)/shard_map/reshape;reshape | solution.py:41
  148.2 1.6 slice.77
  150.8 1.6 fusion.123
  153.2 1.6 fusion.121
  156.7 2.5 %fusion.87 = f32[2,512,128]{2,1,0:T(8,128)S(1)} fusion(f32[2,512,128]{2,1,0:T(8,128)S(1)} %fusion.123, f32[2,512,128]{2,1,0:T(8,128)S(1)} %fusion.15, f32[2,512,128]{2,1,0:T(8,128)S(1)} %copy-done.11, f32[2,512,128]{2,1,0:T(8,128)S(1)} %copy-done.12, f32[2,512,128]{2,1,0:T(8,128)S(1)} %copy-done.13, f32[2,512,128]{2,1,0:T(8,128)S(1)} %copy-done.14, ...), kind=kOutput, calls=%fused_computation.74 | convolution fusion | flops 171442176 | bytes 7172096 | tf_op jit(solution)/shard_map/hqk,khd->hqd/dot_general | solution.py:64
  161.5 12.9 %all_to_all.24 = bf16[8,80,256]{2,1,0:T(8,128)(2,1)S(1)} all-to-all(bf16[8,80,256]{2,1,0:T(8,128)(2,1)S(1)} %all_to_all.18), channel_id=1, replica_groups=mesh['ctx'=32,'head'=8] {'head'}, dimensions={0} | all-to-all | bytes 655360 | tf_op jit(solution)/shard_map/all_to_all | solution.py:106
  (162 shorter events, 38.8 us)
Async XLA Ops:
  0.0 22.5 %copy-start.6 = (bf16[640,256]{1,0:T(8,128)(2,1)S(1)}, bf16[640,256]{1,0:T(8,128)(2,1)}, u32[]{:S(2)}) copy-start(bf16[640,256]{1,0:T(8,128)(2,1)} %param.6) | copy-start | bytes 983044
  0.0 22.6 %copy-start.35 = (bf16[2,16,128]{2,1,0:T(8,128)(2,1)S(1)}, bf16[2,16,128]{2,1,0:T(8,128)(2,1)}, u32[]{:S(2)}) copy-start(bf16[2,16,128]{2,1,0:T(8,128)(2,1)} %param.8) | copy-start | bytes 24580
  1.9 92.6 %collective-permute-start.8 = (bf16[640,256]{0,1:T(8,128)(2,1)}, bf16[640,256]{0,1:T(8,128)(2,1)}, u32[]{:S(2)}, u32[]{:S(2)}) collective-permute-start(bf16[640,256]{0,1:T(8,128)(2,1)} %copy.146), channel_id=1, source_target_pairs={{0,128},{8,136},{16,144},{24,152},{32,160},{40,168},{48,176},{56,1... | collective-permute-start | bytes 983048 | tf_op jit(solution)/shard_map/ppermute | solution.py:25
  9.1 92.2 %collective-permute-start.6 = (bf16[640,256]{0,1:T(8,128)(2,1)}, bf16[640,256]{0,1:T(8,128)(2,1)}, u32[]{:S(2)}, u32[]{:S(2)}) collective-permute-start(bf16[640,256]{0,1:T(8,128)(2,1)} %copy.146), channel_id=1, source_target_pairs={{0,64},{8,72},{16,80},{24,88},{32,96},{40,104},{48,112},{56,120},{... | collective-permute-start | bytes 983048 | tf_op jit(solution)/shard_map/ppermute | solution.py:25
  10.6 93.8 %collective-permute-start.4 = (bf16[640,256]{0,1:T(8,128)(2,1)}, bf16[640,256]{0,1:T(8,128)(2,1)}, u32[]{:S(2)}, u32[]{:S(2)}) collective-permute-start(bf16[640,256]{0,1:T(8,128)(2,1)} %copy.146), channel_id=1, source_target_pairs={{0,32},{8,40},{16,48},{24,56},{32,0},{40,8},{48,16},{56,24},{64,96... | collective-permute-start | bytes 983048 | tf_op jit(solution)/shard_map/ppermute | solution.py:25
  11.6 96.5 %collective-permute-start.2 = (bf16[640,256]{0,1:T(8,128)(2,1)}, bf16[640,256]{0,1:T(8,128)(2,1)S(1)}, u32[]{:S(2)}, u32[]{:S(2)}) collective-permute-start(bf16[640,256]{0,1:T(8,128)(2,1)} %copy.146), channel_id=1, source_target_pairs={{0,16},{8,24},{16,0},{24,8},{32,48},{40,56},{48,32},{56,40},{64,80... | collective-permute-start | bytes 983048 | tf_op jit(solution)/shard_map/ppermute | solution.py:25
  12.0 98.7 %collective-permute-start = (bf16[640,256]{0,1:T(8,128)(2,1)}, bf16[640,256]{0,1:T(8,128)(2,1)S(1)}, u32[]{:S(2)}, u32[]{:S(2)}) collective-permute-start(bf16[640,256]{0,1:T(8,128)(2,1)} %copy.146), channel_id=1, source_target_pairs={{0,8},{8,0},{16,24},{24,16},{32,40},{40,32},{48,56},{56,48},{64,72... | collective-permute-start | bytes 983048 | tf_op jit(solution)/shard_map/ppermute | solution.py:25
  15.0 69.4 %slice-start.1 = ((bf16[640,256]{1,0:T(8,128)(2,1)}), bf16[512,256]{1,0:T(8,128)(2,1)S(1)}, s32[]{:S(2)}) async-start(bf16[640,256]{1,0:T(8,128)(2,1)} %param.5), calls=%async_computation.3 | async-start | bytes 524288 | tf_op jit(solution)/shard_map/slice | solution.py:54
  15.0 130.7 %all-to-all-start = ((bf16[32,40,256]{2,1,0:T(8,128)(2,1)}), bf16[32,40,256]{2,1,0:T(8,128)(2,1)}, u32[]{:S(2)}, u32[]{:S(2)}) async-start(bf16[32,40,256]{2,1,0:T(8,128)(2,1)} %stack.3), calls=%async_computation | async-start | bytes 1310720 | tf_op jit(solution)/shard_map/all_to_all | solution.py:13
  22.5 62.3 %slice-start.2 = ((bf16[640,256]{1,0:T(8,128)(2,1)}), bf16[128,256]{1,0:T(8,128)(2,1)S(1)}, s32[]{:S(2)}) async-start(bf16[640,256]{1,0:T(8,128)(2,1)} %param.5), calls=%async_computation.4 | async-start | bytes 131072 | tf_op jit(solution)/shard_map/slice | solution.py:54
  85.3 27.5 %copy-start.4 = (f32[2,128,640]{2,1,0:T(8,128)}, f32[2,128,640]{2,1,0:T(8,128)S(1)}, u32[]{:S(2)}) copy-start(f32[2,128,640]{2,1,0:T(8,128)S(1)} %get-tuple-element.50) | copy-start | bytes 1966084
  86.7 3.3 %slice-start = ((bf16[1280,256]{1,0:T(8,128)(2,1)}), bf16[256,256]{1,0:T(8,128)(2,1)S(1)}, s32[]{:S(2)}) async-start(bf16[1280,256]{1,0:T(8,128)(2,1)} %copy-done.9), calls=%async_computation.2 | async-start | bytes 262144 | tf_op jit(solution)/shard_map/slice | solution.py:55
  86.7 6.3 %copy-start.7 = (bf16[640,256]{1,0:T(8,128)(2,1)S(1)}, bf16[640,256]{1,0:T(8,128)(2,1)}, u32[]{:S(2)}) copy-start(bf16[640,256]{1,0:T(8,128)(2,1)} %param.7) | copy-start | bytes 983044
  94.5 20.4 %collective-permute-start.9 = (bf16[640,256]{0,1:T(8,128)(2,1)}, bf16[640,256]{0,1:T(8,128)(2,1)S(1)}, u32[]{:S(2)}, u32[]{:S(2)}) collective-permute-start(bf16[640,256]{0,1:T(8,128)(2,1)} %copy.149), channel_id=1, source_target_pairs={{0,128},{8,136},{16,144},{24,152},{32,160},{40,168},{48,176},{56,1... | collective-permute-start | bytes 983048 | tf_op jit(solution)/shard_map/ppermute | solution.py:25
  101.4 26.4 %collective-permute-start.7 = (bf16[640,256]{0,1:T(8,128)(2,1)}, bf16[640,256]{0,1:T(8,128)(2,1)S(1)}, u32[]{:S(2)}, u32[]{:S(2)}) collective-permute-start(bf16[640,256]{0,1:T(8,128)(2,1)} %copy.149), channel_id=1, source_target_pairs={{0,64},{8,72},{16,80},{24,88},{32,96},{40,104},{48,112},{56,120},{... | collective-permute-start | bytes 983048 | tf_op jit(solution)/shard_map/ppermute | solution.py:25
  104.4 26.1 %collective-permute-start.5 = (bf16[640,256]{0,1:T(8,128)(2,1)}, bf16[640,256]{0,1:T(8,128)(2,1)S(1)}, u32[]{:S(2)}, u32[]{:S(2)}) collective-permute-start(bf16[640,256]{0,1:T(8,128)(2,1)} %copy.149), channel_id=1, source_target_pairs={{0,32},{8,40},{16,48},{24,56},{32,0},{40,8},{48,16},{56,24},{64,96... | collective-permute-start | bytes 983048 | tf_op jit(solution)/shard_map/ppermute | solution.py:25
  108.2 24.3 %collective-permute-start.3 = (bf16[640,256]{0,1:T(8,128)(2,1)}, bf16[640,256]{0,1:T(8,128)(2,1)S(1)}, u32[]{:S(2)}, u32[]{:S(2)}) collective-permute-start(bf16[640,256]{0,1:T(8,128)(2,1)} %copy.149), channel_id=1, source_target_pairs={{0,16},{8,24},{16,0},{24,8},{32,48},{40,56},{48,32},{56,40},{64,80... | collective-permute-start | bytes 983048 | tf_op jit(solution)/shard_map/ppermute | solution.py:25
  110.6 45.5 %collective-permute-start.1 = (bf16[640,256]{0,1:T(8,128)(2,1)}, bf16[640,256]{0,1:T(8,128)(2,1)}, u32[]{:S(2)}, u32[]{:S(2)}) collective-permute-start(bf16[640,256]{0,1:T(8,128)(2,1)} %copy.149), channel_id=1, source_target_pairs={{0,8},{8,0},{16,24},{24,16},{32,40},{40,32},{48,56},{56,48},{64,72... | collective-permute-start | bytes 983048 | tf_op jit(solution)/shard_map/ppermute | solution.py:25
  112.8 21.3 %copy-start.29 = (f32[2,128]{1,0:T(2,128)}, f32[2,128]{1,0:T(2,128)S(1)}, u32[]{:S(2)}) copy-start(f32[2,128]{1,0:T(2,128)S(1)} %get-tuple-element.34) | copy-start | bytes 3076
  112.8 21.3 %copy-start.31 = (f32[2,128]{1,0:T(2,128)}, f32[2,128]{1,0:T(2,128)S(1)}, u32[]{:S(2)}) copy-start(f32[2,128]{1,0:T(2,128)S(1)} %get-tuple-element.28) | copy-start | bytes 3076
  112.8 21.3 %copy-start.33 = (f32[2,128]{1,0:T(2,128)}, f32[2,128]{1,0:T(2,128)S(1)}, u32[]{:S(2)}) copy-start(f32[2,128]{1,0:T(2,128)S(1)} %get-tuple-element.29) | copy-start | bytes 3076
  112.8 3.1 %copy-start.32 = (f32[2,512]{1,0:T(2,128)S(1)}, f32[2,512]{1,0:T(2,128)}, u32[]{:S(2)}) copy-start(f32[2,512]{1,0:T(2,128)} %get-tuple-element.53) | copy-start | bytes 12292
  148.2 6.6 %copy-start.1 = (f32[2,1024,512]{2,1,0:T(8,128)S(1)}, f32[2,1024,512]{2,1,0:T(8,128)}, u32[]{:S(2)}) copy-start(f32[2,1024,512]{2,1,0:T(8,128)} %get-tuple-element.56) | copy-start | bytes 12582916
  156.7 4.0 %copy-start.23 = (f32[2,640]{1,0:T(2,128)S(1)}, f32[2,640]{1,0:T(2,128)}, u32[]{:S(2)}) copy-start(f32[2,640]{1,0:T(2,128)} %pad_maximum_fusion) | copy-start | bytes 15364
  (32 other events, 68.9 us)
